TPU v7x, 128 devices: a whole 4x4x4 slice. The times are simulated.
128 devices in a mesh: clip: 8 (over z, core), seq: 16 (over x, y).
Axes of the slice: x: 4, y: 4, z: 4, core: 2. Of those that a mesh axis runs over, the one named last changes fastest.
Arguments:
- query_in: bfloat16 [16384, 4096], P(('clip', 'seq')), parts along dimension 0, may hold values from -12 to 12
- key_in: bfloat16 [16384, 4096], P(('clip', 'seq')), parts along dimension 0, may hold values from -12 to 12
- value_in: bfloat16 [16384, 4096], P(('clip', 'seq')), parts along dimension 0, may hold values from -6 to 6
- grad_out: bfloat16 [16384, 4096], P(('clip', 'seq')), parts along dimension 0, may hold values from -6 to 6
- positions: int32 [3, 16384], P(None, 'clip'), parts along dimension 1, may hold values from 0 to 15, as said below
- block_flags: int32 [128, 16], P('clip'), parts along dimension 0, may hold values from 0 to 1, as said below
- band_ids: int32 [128, 16], P('clip'), parts along dimension 0, may hold values from 0 to 3, as said below
Outputs:
- attn_out: bfloat16 [16384, 4096], P(('clip', 'seq')), parts along dimension 0
- grad_query: bfloat16 [16384, 4096], P(('clip', 'seq')), parts along dimension 0
- grad_key: bfloat16 [16384, 4096], P(('clip', 'seq')), parts along dimension 0
- grad_value: bfloat16 [16384, 4096], P(('clip', 'seq')), parts along dimension 0
There are 8 independent parts, one for each index of `clip`. A program takes and returns all parts, laid end to end along the dimension named above; each array names one. Nothing has to cross between parts.
Inputs may be any that keep to these rules, and one draw needn't show every extreme that they name: positions[0] is the latent frame of a token: tokens come in frames of 256, frame numbers rise strictly from frame to frame and may skip, and the last frame's number is 15; positions[1] and positions[2] are row and column in a square crop, row-major. `block_flags`: diagonal block pairs are always 1. `band_ids`: diagonal block pairs are 0.
All inputs are finite; a program needn't handle non-finite values.
Results may differ from a plain program's by a relative error of at most 0.015.
Values may be sent and summed in bfloat16 or wider, within the bound.
A program may use at most 128 MiB of HBM per device.

v0:
```python
import functools
import math

import jax
import jax.numpy as jnp
import numpy as np
from jax import lax
from jax.experimental import pallas as pl
from jax.experimental.pallas import tpu as pltpu
from jax.sharding import PartitionSpec as P

H = 32
DH = 128
BLK = 128
NPOS = 16
NTK = 2.0
SIDE = 4
HEADS = 2
T = 2048
TQ = 256
CK = 512
NEG = -1e30
SCALE = 1.0 / math.sqrt(DH)
SCALE2 = SCALE * math.log2(math.e)
F32 = jnp.float32
BF16 = jnp.bfloat16
MESH_ID = pl.DeviceIdType.MESH

RING = (1, 3, 2)


def trig_tables():
    third = 2 * (DH // 6)
    dims = (DH - 2 * third, third, third)
    cos_t = np.zeros((3 * NPOS, DH), np.float32)
    sin_t = np.zeros((3 * NPOS, DH), np.float32)
    lane = 0
    for axis, dim in enumerate(dims):
        base = 10000.0 * NTK ** (dim / (dim - 2.0))
        pair = np.arange(dim // 2, dtype=np.float32)
        inverse = np.exp(pair * np.float32(-2.0 * math.log(base) / dim)).astype(np.float32)
        angle = np.arange(NPOS, dtype=np.float32)[:, None] * inverse[None, :]
        c = np.cos(angle.astype(np.float64)).astype(np.float32)
        s = np.sin(angle.astype(np.float64)).astype(np.float32)
        rows = slice(axis * NPOS, (axis + 1) * NPOS)
        cos_t[rows, lane : lane + dim] = np.repeat(c, 2, axis=1)
        sin_t[rows, lane : lane + dim : 2] = -s
        sin_t[rows, lane + 1 : lane + dim : 2] = s
        lane += dim

    def parts(table):
        out, rest = [], table
        for _ in range(3):
            piece = rest.astype(jnp.bfloat16)
            out.append(piece)
            rest = rest - piece.astype(np.float32)
        return out

    return np.stack(parts(cos_t) + parts(sin_t), 0)


def dot(a, b, ca, cb):
    return lax.dot_general(a, b, (((ca,), (cb,)), ((), ())), preferred_element_type=F32)


def swap_pairs(x):
    even = lax.broadcasted_iota(jnp.int32, x.shape, 1) % 2 == 0
    return jnp.where(even, pltpu.roll(x, DH - 1, 1), pltpu.roll(x, 1, 1))


def kernel(
    q_in, k_in, v_in, g_in, pos_ref, flag_ref, band_ref, trig_ref,
    o_out, dq_out, dk_out, dv_out,
    stage, out, relay, land, res, cos_sc, sin_sc, bias, wexp, s_sc, w_all, inv_sc, dk_acc, dv_acc,
    stage_sem, send_sem, recv_sem, own_sem,
):
    clip = lax.axis_index("clip")
    me = lax.axis_index("seq")
    x, y = me // SIDE, me % SIDE
    ins = (q_in, k_in, v_in, g_in)

    def stage_copy(a, n):
        owner, h = n // HEADS, n % HEADS
        return pltpu.make_async_copy(
            ins[a].at[:, n * DH : (n + 1) * DH],
            stage.at[a, owner // SIDE, owner % SIDE, h],
            stage_sem.at[a, n],
        )


    def bring(h, pair):
        for a in pair:
            for n in range(h, H, HEADS):
                stage_copy(a, n).start()

    def brought(h, pair):
        for a in pair:
            for n in range(h, H, HEADS):
                stage_copy(a, n).wait()

    first, second = (0, 1), (2, 3)
    barrier = pltpu.get_barrier_semaphore()
    for j in RING:
        for peer in (((x + j) % SIDE) * SIDE + y, x * SIDE + (y + j) % SIDE):
            pl.semaphore_signal(barrier, inc=1, device_id=(clip, peer), device_id_type=MESH_ID)
    bring(0, first)
    pl.semaphore_wait(barrier, 2 * len(RING))

    def ends(way, h, a, leg, along_x, idx):
        if leg == 0:
            if way == 0:
                src = stage.at[a, idx, :, h] if along_x else stage.at[a, :, idx, h]
            else:
                src = res.at[h, a, idx] if along_x else res.at[h, a, :, idx]
            return src, relay.at[way, h, a, :, x if along_x else y]
        src = relay.at[way, h, a, idx]
        if way == 0:
            return src, land.at[h, a, x] if along_x else land.at[h, a, :, y]
        return src, out.at[a, x, :, h] if along_x else out.at[a, :, y, h]

    def copies(way, h, a, leg):
        along_x = (a % 2 == 0) == (leg == 0)
        made = []
        for n, j in enumerate(RING):
            idx = (x + j) % SIDE if along_x else (y + j) % SIDE
            peer = idx * SIDE + y if along_x else x * SIDE + idx
            src, dst = ends(way, h, a, leg, along_x, idx)
            made.append(
                pltpu.make_async_remote_copy(
                    src_ref=src,
                    dst_ref=dst,
                    send_sem=send_sem.at[way, h, a, leg, n],
                    recv_sem=recv_sem.at[way, h, a, leg, n],
                    device_id=(clip, peer),
                    device_id_type=MESH_ID,
                )
            )
        return made

    def own_copy(way, h, a, leg):
        along_x = (a % 2 == 0) == (leg == 0)
        src, dst = ends(way, h, a, leg, along_x, x if along_x else y)
        return pltpu.make_async_copy(src, dst, own_sem.at[way, h, a, leg])

    def start(way, h, pair, leg):
        made = [copies(way, h, a, leg) for a in pair]
        for n in range(len(RING)):
            for remote in made:
                remote[n].start()
        for a in pair:
            own_copy(way, h, a, leg).start()

    def arrived(way, h, pair, leg):
        for a in pair:
            for c in copies(way, h, a, leg):
                c.wait_recv()
            own_copy(way, h, a, leg).wait()

    bring(0, second)
    brought(0, first)
    start(0, 0, first, 0)
    brought(0, second)
    start(0, 0, second, 0)
    bring(1, first + second)

    value = lax.broadcasted_iota(jnp.int32, (3 * NPOS, TQ), 0)

    def table_rows(t, _):
        at = pl.ds(pl.multiple_of(t * TQ, TQ), TQ)
        p = pos_ref[:, at]
        want = jnp.where(
            value < NPOS, p[0:1, :], jnp.where(value < 2 * NPOS, p[1:2, :] + NPOS, p[2:3, :] + 2 * NPOS)
        )
        hot = jnp.where(value == want, 1.0, 0.0).astype(BF16)
        cos_sc[at, :] = sum(dot(hot, trig_ref[j], 0, 0) for j in range(3))
        sin_sc[at, :] = sum(dot(hot, trig_ref[3 + j], 0, 0) for j in range(3))
        return 0

    lax.fori_loop(0, T // TQ, table_rows, 0)

    blocks = T // BLK
    band = band_ref[...]
    width = jnp.where(band == 0, 128.0, jnp.where(band == 1, 64.0, jnp.where(band == 2, 32.0, 16.0)))
    width = jnp.where(flag_ref[...] == 1, width, 0.0).astype(BF16)
    spread = lax.broadcasted_iota(jnp.int32, (blocks, T), 0) == (
        lax.broadcasted_iota(jnp.int32, (blocks, T), 1) // BLK
    )
    wexp[...] = dot(width, jnp.where(spread, 1.0, 0.0).astype(BF16), 1, 0)
    apart = jnp.abs(
        lax.broadcasted_iota(jnp.int32, (BLK, BLK), 0) - lax.broadcasted_iota(jnp.int32, (BLK, BLK), 1)
    ).astype(F32)

    def bias_rows(t, _):
        reach = wexp[pl.ds(t, 1), :]
        at = pl.ds(pl.multiple_of(t * BLK, BLK), BLK)
        for j in range(blocks):
            bias[at, j * BLK : (j + 1) * BLK] = jnp.where(
                apart < reach[:, j * BLK : (j + 1) * BLK], 0.0, NEG
            ).astype(BF16)
        return 0

    lax.fori_loop(0, blocks, bias_rows, 0)

    arrived(0, 0, first, 0)
    start(0, 0, first, 1)
    arrived(0, 0, second, 0)
    start(0, 0, second, 1)
    brought(1, first + second)
    start(0, 1, first, 0)
    start(0, 1, second, 0)

    def tile_of(ref, h, a, t):
        return ref.at[h, a, t // 2, pl.ds((t % 2) * 2, 2)]

    def load_tile(ref, h, a, t):
        return tile_of(ref, h, a, t)[...].reshape(TQ, DH)

    def chunk(h, a, c):
        return land[h, a, c].reshape(CK, DH)

    def rows_at(t):
        return pl.ds(pl.multiple_of(t * TQ, TQ), TQ)

    def run_hooks(hooks, t):
        for when, job in hooks.items():
            @pl.when(t == when)
            def _(job=job):
                job()

    def scores_pass(h, hooks):
        arrived(0, h, first, 1)

        def turn(t, _):
            at = rows_at(t)
            for a in (0, 1):
                v = load_tile(land, h, a, t).astype(F32)
                v = v * cos_sc[at, :] + swap_pairs(v) * sin_sc[at, :]
                tile_of(land, h, a, t)[...] = v.astype(BF16).reshape(2, BLK, DH)
            return 0

        lax.fori_loop(0, T // TQ, turn, 0)

        def tile(t, _):
            run_hooks(hooks, t)
            at = rows_at(t)
            q = load_tile(land, h, 0, t)
            high = jnp.full((TQ, 128), -jnp.inf, F32)
            for c in range(T // CK):
                cs = pl.ds(c * CK, CK)
                s = dot(q, chunk(h, 1, c), 1, 1) + bias[at, cs].astype(F32)
                s_sc[:, cs] = s
                for j in range(CK // 128):
                    high = jnp.maximum(high, s[:, j * 128 : (j + 1) * 128])
            m = jnp.max(high, axis=1, keepdims=True)
            total = jnp.zeros((TQ, 128), F32)
            for c in range(T // CK):
                cs = pl.ds(c * CK, CK)
                w = jnp.exp2((s_sc[:, cs] - m) * SCALE2)
                for j in range(CK // 128):
                    total = total + w[:, j * 128 : (j + 1) * 128]
                w_all[at, cs] = w.astype(BF16)
            inv = 1.0 / jnp.sum(total, axis=1, keepdims=True)
            inv_sc[at, :] = jnp.broadcast_to(inv, (TQ, 128))
            return 0

        lax.fori_loop(0, T // TQ, tile, 0)

    def grads_pass(h, hooks):
        arrived(0, h, second, 1)
        dk_acc[...] = jnp.zeros_like(dk_acc)
        dv_acc[...] = jnp.zeros_like(dv_acc)

        def tile(t, _):
            run_hooks(hooks, t)
            at = rows_at(t)
            q = load_tile(land, h, 0, t)
            g = load_tile(land, h, 3, t)
            inv = inv_sc[at, :]
            o = jnp.zeros((TQ, DH), F32)
            for c in range(T // CK):
                o = o + dot(w_all[at, pl.ds(c * CK, CK)], chunk(h, 2, c), 1, 0)
            gf = g.astype(F32)
            ob = (o * inv).astype(BF16)
            tile_of(res, h, 0, t)[...] = ob.reshape(2, BLK, DH)
            gn = gf * inv
            delta = jnp.sum(gn * ob.astype(F32), axis=1, keepdims=True)
            gn = gn.astype(BF16)
            gt, qt = gn.T, q.T
            dq = jnp.zeros((TQ, DH), F32)
            for c in range(T // CK):
                cs = pl.ds(c * CK, CK)
                dp = dot(gn, chunk(h, 2, c), 1, 1)
                wb = w_all[at, cs]
                ds = (wb.astype(F32) * (dp - delta)).astype(BF16)
                dq = dq + dot(ds, chunk(h, 1, c), 1, 0)
                dv_acc[:, cs] += dot(gt, wb, 1, 0)
                dk_acc[:, cs] += dot(qt, ds, 1, 0)
            dq = dq * SCALE
            dq = dq * cos_sc[at, :] - swap_pairs(dq) * sin_sc[at, :]
            tile_of(res, h, 1, t)[...] = dq.astype(BF16).reshape(2, BLK, DH)
            return 0

        lax.fori_loop(0, T // TQ, tile, 0)
        for t in range(T // TQ):
            cs = pl.ds(t * TQ, TQ)
            dk = dk_acc[:, cs].T * SCALE
            dk = dk * cos_sc[cs, :] - swap_pairs(dk) * sin_sc[cs, :]
            tile_of(res, h, 2, t)[...] = dk.astype(BF16).reshape(2, BLK, DH)
            tile_of(res, h, 3, t)[...] = dv_acc[:, cs].T.astype(BF16).reshape(2, BLK, DH)

    def forward(way, h, pair):
        def job():
            arrived(way, h, pair, 0)
            start(way, h, pair, 1)

        return job

    scores_pass(0, {})
    grads_pass(0, {2: forward(0, 1, first), 4: forward(0, 1, second)})
    start(1, 0, first, 0)
    start(1, 0, second, 0)
    scores_pass(1, {6: forward(1, 0, first)})
    grads_pass(1, {2: forward(1, 0, second)})
    start(1, 1, first, 0)
    start(1, 1, second, 0)
    forward(1, 1, first)()
    forward(1, 1, second)()

    outs = (o_out, dq_out, dk_out, dv_out)
    for h in range(HEADS):
        for pair in (first, second):
            arrived(1, h, pair, 1)
            for a in pair:
                for n in range(h, H, HEADS):
                    owner = n // HEADS
                    outs[a][:, n * DH : (n + 1) * DH] = out[a, owner // SIDE, owner % SIDE, h]
    for h in range(HEADS):
        for way in range(2):
            for a in range(4):
                for leg in range(2):
                    for c in copies(way, h, a, leg):
                        c.wait_send()


def write_out(o, dq, dk, dv, o_out, dq_out, dk_out, dv_out, sem):
    made = [
        pltpu.make_async_copy(src, dst, sem.at[n])
        for n, (src, dst) in enumerate(((o, o_out), (dq, dq_out), (dk, dk_out), (dv, dv_out)))
    ]
    for c in made:
        c.start()
    for c in made:
        c.wait()


def body(query_in, key_in, value_in, grad_out, positions, block_flags, band_ids):
    shape = query_in.shape
    any_spec = pl.BlockSpec(memory_space=pl.ANY)
    vmem = pl.BlockSpec(memory_space=pltpu.VMEM)
    hops = pltpu.SemaphoreType.DMA((2, HEADS, 4, 2, len(RING)))
    grid = (HEADS, 4, SIDE, SIDE, BLK, DH)
    results = pl.pallas_call(
        kernel,
        name="attention_exchange",
        out_shape=[pltpu.VMEM(shape, BF16)] * 4,
        in_specs=[any_spec] * 4 + [vmem] * 4,
        out_specs=[vmem] * 4,
        scratch_shapes=[
            pltpu.VMEM((4, SIDE, SIDE, HEADS, BLK, DH), BF16),
            pltpu.VMEM((4, SIDE, SIDE, HEADS, BLK, DH), BF16),
            pltpu.VMEM((2,) + grid, BF16),
            pltpu.VMEM(grid, BF16),
            pltpu.VMEM(grid, BF16),
            pltpu.VMEM((T, DH), F32),
            pltpu.VMEM((T, DH), F32),
            pltpu.VMEM((T, T), BF16),
            pltpu.VMEM((T // BLK, T), F32),
            pltpu.VMEM((TQ, T), F32),
            pltpu.VMEM((T, T), BF16),
            pltpu.VMEM((T, 128), F32),
            pltpu.VMEM((DH, T), F32),
            pltpu.VMEM((DH, T), F32),
            pltpu.SemaphoreType.DMA((4, H)),
            hops,
            hops,
            pltpu.SemaphoreType.DMA((2, HEADS, 4, 2)),
        ],
        compiler_params=pltpu.CompilerParams(
            collective_id=0, has_side_effects=True, vmem_limit_bytes=56000 * 1024
        ),
    )(query_in, key_in, value_in, grad_out, positions, block_flags, band_ids, jnp.asarray(trig_tables()))
    return tuple(
        pl.pallas_call(
            write_out,
            name="write_out",
            out_shape=[jax.ShapeDtypeStruct(shape, BF16)] * 4,
            in_specs=[vmem] * 4,
            out_specs=[any_spec] * 4,
            scratch_shapes=[pltpu.SemaphoreType.DMA((4,))],
            compiler_params=pltpu.CompilerParams(vmem_limit_bytes=4 * 1024 * 1024),
        )(*(pltpu.with_memory_space_constraint(r, pltpu.VMEM) for r in results))
    )


def solution(mesh):
    spec = P(("clip", "seq"), None)
    return jax.shard_map(
        body,
        mesh=mesh,
        in_specs=(spec, spec, spec, spec, P(None, "clip"), P("clip", None), P("clip", None)),
        out_specs=(spec, spec, spec, spec),
        check_vma=False,
    )
```

profile of v0, /device:TPU:68, one launch (start us, length us, event | category | flops | bytes accessed | tf_op | source)
XLA Modules:
  0.0 104.1 jit_solution(8061306376278241344)
XLA Ops:
  0.6 101.4 %attention_exchange.1 = (bf16[128,4096]{1,0:T(8,128)(2,1)S(1)}, bf16[128,4096]{1,0:T(8,128)(2,1)S(1)}, bf16[128,4096]{1,0:T(8,128)(2,1)S(1)}, bf16[128,4096]{1,0:T(8,128)(2,1)S(1)}) custom-call(bf16[128,4096]{1,0:T(8,128)(2,1)} %q_in.1, bf16[128,4096]{1,0:T(8,128)(2,1)} %k_in.1, bf16[128,4096]{1,0:T(8,128)(2,1)} %v_in.1, bf16[128,4096]{1,0:T(8,128)(2,1)} %g_in.1, ...), custom_call_target="tpu_custom_call" | custom-call | tf_op jit(solution)/shard_map/attention_exchange/pallas_call | solution.py:362
  102.0 2.0 %write_out.1 = (bf16[128,4096]{1,0:T(8,128)(2,1)}, bf16[128,4096]{1,0:T(8,128)(2,1)}, bf16[128,4096]{1,0:T(8,128)(2,1)}, bf16[128,4096]{1,0:T(8,128)(2,1)}) custom-call(bf16[128,4096]{1,0:T(8,128)(2,1)S(1)} %get-tuple-element.8.o, bf16[128,4096]{1,0:T(8,128)(2,1)S(1)} %get-tuple-element.9.dq, bf16[128,4096]{1,0:T(8,128)(2,1)S(1)} %get-tuple-element.10.dk, ...), custom_call_target="tpu_custom_call" | custom-call | tf_op jit(solution)/shard_map/write_out/pallas_call | solution.py:393
where the time goes:
time: 105 us; the launch traced here: 104 us
  Pallas kernels  103 us (98%)
    pallas_call x1, Pallas kernels, body(): pl.pallas_call(kernel, name='attention_exchange', out_shape=[pltpu.VMEM(s...  101 us

commit v1 on v0

--- a/solution.py
+++ b/solution.py
@@ -69,10 +69,11 @@
 
 
 def kernel(
-    q_in, k_in, v_in, g_in, pos_ref, flag_ref, band_ref, trig_ref,
+    q_in, k_in, v_in, g_in, pos_in, flag_in, band_in, trig_in,
     o_out, dq_out, dk_out, dv_out,
     stage, out, relay, land, res, cos_sc, sin_sc, bias, wexp, s_sc, w_all, inv_sc, dk_acc, dv_acc,
-    stage_sem, send_sem, recv_sem, own_sem,
+    pos_ref, flag_ref, band_ref, trig_ref,
+    stage_sem, send_sem, recv_sem, own_sem, small_sem,
 ):
     clip = lax.axis_index("clip")
     me = lax.axis_index("seq")
@@ -104,6 +105,14 @@
         for peer in (((x + j) % SIDE) * SIDE + y, x * SIDE + (y + j) % SIDE):
             pl.semaphore_signal(barrier, inc=1, device_id=(clip, peer), device_id_type=MESH_ID)
     bring(0, first)
+    small = [
+        pltpu.make_async_copy(src, dst, small_sem.at[n])
+        for n, (src, dst) in enumerate(
+            ((pos_in, pos_ref), (flag_in, flag_ref), (band_in, band_ref), (trig_in, trig_ref))
+        )
+    ]
+    for c in small:
+        c.start()
     pl.semaphore_wait(barrier, 2 * len(RING))
 
     def ends(way, h, a, leg, along_x, idx):
@@ -162,6 +171,9 @@
     brought(0, second)
     start(0, 0, second, 0)
     bring(1, first + second)
+
+    for c in small:
+        c.wait()
 
     value = lax.broadcasted_iota(jnp.int32, (3 * NPOS, TQ), 0)
 
@@ -316,11 +328,11 @@
         return job
 
     scores_pass(0, {})
-    grads_pass(0, {2: forward(0, 1, first), 4: forward(0, 1, second)})
+    grads_pass(0, {3: forward(0, 1, first), 5: forward(0, 1, second)})
     start(1, 0, first, 0)
     start(1, 0, second, 0)
-    scores_pass(1, {6: forward(1, 0, first)})
-    grads_pass(1, {2: forward(1, 0, second)})
+    scores_pass(1, {7: forward(1, 0, first)})
+    grads_pass(1, {3: forward(1, 0, second)})
     start(1, 1, first, 0)
     start(1, 1, second, 0)
     forward(1, 1, first)()
@@ -357,13 +369,14 @@
     shape = query_in.shape
     any_spec = pl.BlockSpec(memory_space=pl.ANY)
     vmem = pl.BlockSpec(memory_space=pltpu.VMEM)
+    trig = jnp.asarray(trig_tables())
     hops = pltpu.SemaphoreType.DMA((2, HEADS, 4, 2, len(RING)))
     grid = (HEADS, 4, SIDE, SIDE, BLK, DH)
     results = pl.pallas_call(
         kernel,
         name="attention_exchange",
         out_shape=[pltpu.VMEM(shape, BF16)] * 4,
-        in_specs=[any_spec] * 4 + [vmem] * 4,
+        in_specs=[any_spec] * 8,
         out_specs=[vmem] * 4,
         scratch_shapes=[
             pltpu.VMEM((4, SIDE, SIDE, HEADS, BLK, DH), BF16),
@@ -380,15 +393,20 @@
             pltpu.VMEM((T, 128), F32),
             pltpu.VMEM((DH, T), F32),
             pltpu.VMEM((DH, T), F32),
+            pltpu.VMEM(positions.shape, jnp.int32),
+            pltpu.VMEM(block_flags.shape, jnp.int32),
+            pltpu.VMEM(band_ids.shape, jnp.int32),
+            pltpu.VMEM(trig.shape, BF16),
             pltpu.SemaphoreType.DMA((4, H)),
             hops,
             hops,
             pltpu.SemaphoreType.DMA((2, HEADS, 4, 2)),
+            pltpu.SemaphoreType.DMA((4,)),
         ],
         compiler_params=pltpu.CompilerParams(
             collective_id=0, has_side_effects=True, vmem_limit_bytes=56000 * 1024
         ),
-    )(query_in, key_in, value_in, grad_out, positions, block_flags, band_ids, jnp.asarray(trig_tables()))
+    )(query_in, key_in, value_in, grad_out, positions, block_flags, band_ids, trig)
     return tuple(
         pl.pallas_call(
             write_out,

time: 105 us -> 104 us (level)
  Pallas kernels: 103 us -> 101 us
    pallas_call x1, Pallas kernels: 101 us -> 99.4 us  [body(): pl.pallas_call(kernel, name='attention_exchange', out_shape=[pltpu.VMEM(s...]
where the time goes in v1:
time: 104 us; the launch traced here: 102 us
  Pallas kernels  101 us (97%)
    pallas_call x1, Pallas kernels, body(): pl.pallas_call(kernel, name='attention_exchange', out_shape=[pltpu.VMEM(s...  99.4 us

profile of v1, /device:TPU:68, one launch (start us, length us, event | category | flops | bytes accessed | tf_op | source)
XLA Modules:
  0.0 102.0 jit_solution(12438854744946436736)
XLA Ops:
  0.6 99.4 %attention_exchange.1 = (bf16[128,4096]{1,0:T(8,128)(2,1)S(1)}, bf16[128,4096]{1,0:T(8,128)(2,1)S(1)}, bf16[128,4096]{1,0:T(8,128)(2,1)S(1)}, bf16[128,4096]{1,0:T(8,128)(2,1)S(1)}) custom-call(bf16[128,4096]{1,0:T(8,128)(2,1)} %q_in.1, bf16[128,4096]{1,0:T(8,128)(2,1)} %k_in.1, bf16[128,4096]{1,0:T(8,128)(2,1)} %v_in.1, bf16[128,4096]{1,0:T(8,128)(2,1)} %g_in.1, ...), custom_call_target="tpu_custom_call" | custom-call | tf_op jit(solution)/shard_map/attention_exchange/pallas_call | solution.py:375
  100.0 2.0 %write_out.1 = (bf16[128,4096]{1,0:T(8,128)(2,1)}, bf16[128,4096]{1,0:T(8,128)(2,1)}, bf16[128,4096]{1,0:T(8,128)(2,1)}, bf16[128,4096]{1,0:T(8,128)(2,1)}) custom-call(bf16[128,4096]{1,0:T(8,128)(2,1)S(1)} %get-tuple-element.8.o, bf16[128,4096]{1,0:T(8,128)(2,1)S(1)} %get-tuple-element.9.dq, bf16[128,4096]{1,0:T(8,128)(2,1)S(1)} %get-tuple-element.10.dk, ...), custom_call_target="tpu_custom_call" | custom-call | tf_op jit(solution)/shard_map/write_out/pallas_call | solution.py:411

commit v2 on v1

--- a/solution.py
+++ b/solution.py
@@ -319,6 +319,8 @@
             dk = dk * cos_sc[cs, :] - swap_pairs(dk) * sin_sc[cs, :]
             tile_of(res, h, 2, t)[...] = dk.astype(BF16).reshape(2, BLK, DH)
             tile_of(res, h, 3, t)[...] = dv_acc[:, cs].T.astype(BF16).reshape(2, BLK, DH)
+            if t == 1:
+                start(1, h, first, 0)
 
     def forward(way, h, pair):
         def job():
@@ -329,11 +331,9 @@
 
     scores_pass(0, {})
     grads_pass(0, {3: forward(0, 1, first), 5: forward(0, 1, second)})
-    start(1, 0, first, 0)
     start(1, 0, second, 0)
     scores_pass(1, {7: forward(1, 0, first)})
     grads_pass(1, {3: forward(1, 0, second)})
-    start(1, 1, first, 0)
     start(1, 1, second, 0)
     forward(1, 1, first)()
     forward(1, 1, second)()

time: 104 us -> 103 us (level)
  no operation moved by 1% of the time
where the time goes in v2:
time: 103 us; the launch traced here: 102 us
  Pallas kernels  101 us (98%)
    pallas_call x1, Pallas kernels, body(): pl.pallas_call(kernel, name='attention_exchange', out_shape=[pltpu.VMEM(s...  98.9 us

profile of v2, /device:TPU:68, one launch (start us, length us, event | category | flops | bytes accessed | tf_op | source)
XLA Modules:
  0.0 101.6 jit_solution(7410900316926758903)
XLA Ops:
  0.6 98.9 %attention_exchange.1 = (bf16[128,4096]{1,0:T(8,128)(2,1)S(1)}, bf16[128,4096]{1,0:T(8,128)(2,1)S(1)}, bf16[128,4096]{1,0:T(8,128)(2,1)S(1)}, bf16[128,4096]{1,0:T(8,128)(2,1)S(1)}) custom-call(bf16[128,4096]{1,0:T(8,128)(2,1)} %q_in.1, bf16[128,4096]{1,0:T(8,128)(2,1)} %k_in.1, bf16[128,4096]{1,0:T(8,128)(2,1)} %v_in.1, bf16[128,4096]{1,0:T(8,128)(2,1)} %g_in.1, ...), custom_call_target="tpu_custom_call" | custom-call | tf_op jit(solution)/shard_map/attention_exchange/pallas_call | solution.py:375
  99.5 2.0 %write_out.1 = (bf16[128,4096]{1,0:T(8,128)(2,1)}, bf16[128,4096]{1,0:T(8,128)(2,1)}, bf16[128,4096]{1,0:T(8,128)(2,1)}, bf16[128,4096]{1,0:T(8,128)(2,1)}) custom-call(bf16[128,4096]{1,0:T(8,128)(2,1)S(1)} %get-tuple-element.8.o, bf16[128,4096]{1,0:T(8,128)(2,1)S(1)} %get-tuple-element.9.dq, bf16[128,4096]{1,0:T(8,128)(2,1)S(1)} %get-tuple-element.10.dk, ...), custom_call_target="tpu_custom_call" | custom-call | tf_op jit(solution)/shard_map/write_out/pallas_call | solution.py:411
